TPU v7x, 256 devices: a whole 4x4x8 slice. The times are simulated.
256 devices in a mesh: blk: 32 (over y, x, core), col: 8 (over z).
Axes of the slice: x: 4, y: 4, z: 8, core: 2. Of those that a mesh axis runs over, the one named last changes fastest.
Arguments:
- src_feat: bfloat16 [64, 1024, 256], P('blk', 'col'), may hold values from -40 to 40
- tgt_feat: bfloat16 [64, 1024, 256], P('blk', 'col'), may hold values from -40 to 40
- src_mass: bfloat16 [64, 1024], P('blk', 'col'), may hold values from 0.5 to 2
- tgt_mass: bfloat16 [64, 1024], P('blk', 'col'), may hold values from 0.5 to 2
- candidates: int32 [64, 8], P('blk'), may hold values from 0 to 63, as said below
- counts: int32 [64], P('blk'), may hold values from 1 to 8, as said below
- tgt_home: int32 [64], replicated, may hold values from 0 to 63, each once
Outputs:
- src_aligned: bfloat16 [64, 1024, 256], P('blk', 'col')
- tgt_aligned: bfloat16 [64, 1024, 256], P('blk', 'col')
Inputs may be any that keep to these rules, and one draw needn't show every extreme that they name: `candidates`: each row's 8 entries are distinct; the first counts[i] of row i are live, the others are not used; every target block number is among the live entries of some row. `counts`: the 2 blocks of one index of blk hold at most 12 live slots together, and the blocks of some index hold exactly 12. A permutation: target block number j is stored as block tgt_home[j] of tgt_feat and tgt_mass.
All inputs are finite; a program needn't handle non-finite values.
Results may differ from a plain program's by a relative error of at most 0.017.
Values may be sent and summed in bfloat16 or wider, within the bound.
No kernel may reach another device: no remote copies, remote signals or barrier semaphores. Data moves between devices by JAX's collectives and lax.ppermute only.
A program may use at most 64 MiB of HBM per device.

v0:
```python
import jax
import jax.numpy as jnp
from jax import lax
from jax.sharding import PartitionSpec as P

ITERS = 2
PAIRS = 12
score_offset = 0.3
softness_level = 0.02
epsilon = 1e-06
highest = lax.Precision.HIGHEST
slot_group = 4


def unit_rows(features):
    values = features.astype(jnp.float32)
    inverse = lax.rsqrt(jnp.mean(values * values, axis=-1, keepdims=True) + epsilon)
    return (values * inverse).astype(jnp.bfloat16)


def grouped(values_in):
    return values_in.reshape((values_in.shape[0] // slot_group, slot_group) + values_in.shape[1:])


def kernels(src_blocks, tgt_tiles):
    feature_total = src_blocks.shape[-1]
    score_matrix = jnp.einsum(
        "sbw,stw->sbt", src_blocks, tgt_tiles, preferred_element_type=jnp.float32
    )
    return jnp.exp((score_matrix / feature_total - score_offset) / softness_level)


def local(src_feat, tgt_feat, src_mass, tgt_mass, candidates, counts, tgt_home):
    local_blocks, sub_rows, feature_total = src_feat.shape
    slot_max = candidates.shape[1]
    block_count = tgt_home.shape[0]
    src_full, mass_full = (
        lax.all_gather(src_feat, "col", axis=1, tiled=True),
        lax.all_gather(src_mass, "col", axis=1, tiled=True),
    )
    full_rows = src_full.shape[1]
    src_unit = unit_rows(src_full)
    src_weight = mass_full.astype(jnp.float32)
    block_ids = jnp.arange(block_count, dtype=jnp.int32)
    local_ids = jnp.arange(local_blocks, dtype=jnp.int32)
    home_flat = jnp.sum(
        jnp.where(candidates.reshape(-1)[:, None] == block_ids[None, :], tgt_home[None, :], 0),
        axis=1,
    )
    slot_count = PAIRS
    block_ends = jnp.cumsum(counts)
    block_starts = block_ends - counts
    position = jnp.arange(slot_count, dtype=jnp.int32)
    src_of = jnp.minimum(
        jnp.sum((position[:, None] >= block_ends[None, :]).astype(jnp.int32), axis=1),
        local_blocks - 1,
    )
    owner_hot = src_of[:, None] == local_ids[None, :]
    within = position - jnp.sum(jnp.where(owner_hot, block_starts[None, :], 0), axis=1)
    alive_flag = position < block_ends[-1]
    flat_index = src_of * slot_max + jnp.clip(within, 0, slot_max - 1)
    flat_ids = jnp.arange(local_blocks * slot_max, dtype=jnp.int32)
    tgt_of = jnp.sum(
        jnp.where(flat_index[:, None] == flat_ids[None, :], home_flat[None, :], 0), axis=1
    )
    alive = alive_flag.astype(jnp.float32)
    masses = lax.all_gather(tgt_mass, "blk", axis=0, tiled=True).astype(jnp.float32)
    shard_piece = lax.all_gather(tgt_feat, "blk", axis=0, tiled=True)
    piece_rows = shard_piece.shape[0]
    chooser = (tgt_of[:, None] == jnp.arange(piece_rows, dtype=jnp.int32)[None, :]).astype(
        jnp.bfloat16
    )
    picked = jnp.einsum("sm,mtw->stw", chooser, shard_piece, preferred_element_type=jnp.float32)
    tiles_raw = picked.astype(jnp.bfloat16)
    tiles_unit = unit_rows(tiles_raw)
    pick_float = (tgt_of[:, None] == block_ids[None, :]).astype(jnp.float32)
    src_onehot = (src_of[:, None] == local_ids[None, :]).astype(jnp.float32)
    unit_groups = grouped(tiles_unit)
    raw_groups = grouped(tiles_raw)
    src_groups = grouped(src_of)
    active_group_flags = grouped(alive)
    group_indicator = grouped(src_onehot)
    kernel_elements = (unit_groups, src_groups)

    def tile_of(item):
        return kernels(jnp.take(src_unit, item[1], axis=0), item[0])

    def slot_scale_factors(column_scaling_vector):
        return grouped(
            jnp.einsum("sn,nt->st", pick_float, column_scaling_vector, precision=highest)
        )

    def row_pass(column_scaling_vector):

        def row_step(running, entry):
            item, alive_slots, onehot_slots, v_rows = entry
            kernel_tile = tile_of(item)
            row_part = (
                jnp.einsum("sbt,st->sb", kernel_tile, v_rows, precision=highest)
                * alive_slots[:, None]
            )
            return (
                running + jnp.einsum("sp,sb->pb", onehot_slots, row_part, precision=highest),
                None,
            )

        start_rows = jnp.zeros((local_blocks, full_rows), jnp.float32)
        result, _ = lax.scan(
            row_step,
            start_rows,
            (
                kernel_elements,
                active_group_flags,
                group_indicator,
                slot_scale_factors(column_scaling_vector),
            ),
        )
        return result

    def col_pass(scaling_u):

        def col_step(running, entry):
            item, src_ids, alive_slots = entry
            kernel_tile = tile_of(item)
            u_rows = jnp.take(scaling_u, src_ids, axis=0)
            col_part = (
                jnp.einsum("sb,sbt->st", u_rows, kernel_tile, precision=highest)
                * alive_slots[:, None]
            )
            return (running, col_part)

        _, col_parts = lax.scan(
            col_step, jnp.zeros((), jnp.float32), (kernel_elements, src_groups, active_group_flags)
        )
        return jnp.einsum(
            "sn,st->nt", pick_float, col_parts.reshape(slot_count, sub_rows), precision=highest
        )

    column_scaling_vector = jnp.ones((block_count, sub_rows), jnp.float32)
    scaling_u = jnp.ones((local_blocks, full_rows), jnp.float32)
    for iteration in range(ITERS):
        row_sums = lax.psum(row_pass(column_scaling_vector), "col")
        scaling_u = src_weight / row_sums
        col_terms = col_pass(scaling_u)
        column_scaling_vector = masses / lax.psum(col_terms.astype(jnp.bfloat16), "blk").astype(
            jnp.float32
        )

    def final_step(running, entry):
        item, raw_tiles, src_ids, alive_slots, onehot_slots, v_rows = entry
        kernel_tile = tile_of(item)
        u_rows = jnp.take(scaling_u, src_ids, axis=0)
        plan = (
            u_rows[:, :, None] * kernel_tile * v_rows[:, None, :] * alive_slots[:, None, None]
        ).astype(jnp.bfloat16)
        toward = jnp.einsum("sbt,stw->sbw", plan, raw_tiles, preferred_element_type=jnp.float32)
        running = running + jnp.einsum("sp,sbw->pbw", onehot_slots, toward, precision=highest)
        back_terms = jnp.einsum(
            "sbt,sbw->stw",
            plan,
            jnp.take(src_full, src_ids, axis=0),
            preferred_element_type=jnp.float32,
        )
        return (running, back_terms)

    start_sums = jnp.zeros((local_blocks, full_rows, feature_total), jnp.float32)
    final_entries = (
        kernel_elements,
        raw_groups,
        src_groups,
        active_group_flags,
        group_indicator,
        slot_scale_factors(column_scaling_vector),
    )
    src_sums, pair_sums = lax.scan(final_step, start_sums, final_entries)
    pair_sums = pair_sums.reshape(slot_count, sub_rows, feature_total)
    src_own = lax.psum_scatter(
        src_sums.astype(jnp.bfloat16), "col", scatter_dimension=1, tiled=True
    ).astype(jnp.float32)
    wanted = (
        jnp.arange(local_blocks * lax.axis_size("blk"), dtype=jnp.int32)[:, None] == tgt_of[None, :]
    ).astype(jnp.float32)
    tgt_own = lax.psum_scatter(
        jnp.einsum("ns,stw->ntw", wanted, pair_sums, precision=highest).astype(jnp.bfloat16),
        "blk",
        scatter_dimension=0,
        tiled=True,
    ).astype(jnp.float32)
    src_aligned = (src_own / src_mass.astype(jnp.float32)[:, :, None]).astype(jnp.bfloat16)
    tgt_aligned = (tgt_own / tgt_mass.astype(jnp.float32)[:, :, None]).astype(jnp.bfloat16)
    return (src_aligned, tgt_aligned)


def solution(mesh):
    in_specs = (
        P("blk", "col", None),
        P("blk", "col", None),
        P("blk", "col"),
        P("blk", "col"),
        P("blk", None),
        P("blk"),
        P(),
    )
    out_specs = (P("blk", "col", None), P("blk", "col", None))
    return jax.shard_map(local, mesh=mesh, in_specs=in_specs, out_specs=out_specs, check_vma=False)
```

profile of v0, /device:TPU:2, one launch (start us, length us, event | category | flops | bytes accessed | tf_op | source)
XLA Modules:
  0.0 660.9 jit_solution(15419486938049489401)
XLA Ops:
  13.0 19.3 %all_gather.12 = bf16[2,1024]{1,0:T(2,128)(2,1)S(1)} all-gather(bf16[2,128]{1,0:T(2,128)(2,1)} %param.23), channel_id=1, replica_groups=mesh['blk'=32,'col'=8] {'col'}, dimensions={1}, use_global_device_ids=true | all-gather | bytes 4608 | tf_op jit(solution)/shard_map/all_gather | solution.py:39
  32.3 21.5 %all-gather = bf16[32,2,128]{2,1,0:T(2,128)(2,1)S(1)} all-gather(bf16[1,2,128]{2,1,0:T(2,128)(2,1)} %bitcast.188), channel_id=1, replica_groups=mesh['blk'=32,'col'=8] {'blk'}, dimensions={0}, use_global_device_ids=true | all-gather | bytes 16896 | tf_op jit(solution)/shard_map/all_gather | solution.py:67
  54.7 1.6 fusion.129
  56.3 1.6 fusion.130
  57.9 45.0 %all-gather.6.cloned.1.call-done = bf16[64,128,256]{2,1,0:T(8,128)(2,1)} async-done(((bf16[2,128,256]{2,1,0:T(8,128)(2,1)}), bf16[64,128,256]{2,1,0:T(8,128)(2,1)}) %all-gather.6.cloned.1.call-update) | async-done | bytes 4194320 | tf_op jit(solution)/shard_map/all_gather | solution.py:68
  102.9 4.6 fusion.131
  110.5 14.7 %while.67 = (s32[]{:T(128)}, f32[2,1024]{1,0:T(2,128)S(1)}, f32[3,4,2]{1,2,0:T(2,128)S(1)}, s32[3,4]{1,0:T(4,128)S(1)}, bf16[2,1024,256]{2,1,0:T(8,128)(2,1)S(1)...) while((s32[]{:T(128)}, f32[2,1024]{1,0:T(2,128)S(1)}, ...), condition=%wide.region_8.10_spmd.clone, body=%wide.region_7.9_spmd.clone.sunk | while | flops 277455904 | bytes 10809075 | solution.py:108
  111.2 1.7 fusion.222
  112.9 2.2 fusion.223
  116.1 1.7 fusion.222
  117.9 2.2 fusion.223
  121.1 1.7 fusion.222
  122.8 2.2 fusion.223
  125.2 17.7 %psum.28 = f32[2,1024]{1,0:T(2,128)S(1)} all-reduce(f32[2,1024]{1,0:T(2,128)S(1)} %get-tuple-element.534), channel_id=1, replica_groups=mesh['blk'=32,'col'=8] {'col'}, use_global_device_ids=true, to_apply=%region_9.11 | all-reduce | flops 2048 | bytes 16384 | tf_op jit(solution)/shard_map/psum | solution.py:142
  143.0 13.8 %while.65 = (s32[]{:T(128)}, f32[3,4,128]{2,1,0:T(4,128)S(1)}, s32[3,4]{1,0:T(4,128)S(1)}, f32[2,1024]{1,0:T(2,128)S(1)}, bf16[2,1024,256]{2,1,0:T(8,128)(2,1)S(...) while((s32[]{:T(128)}, f32[3,4,128]{2,1,0:T(4,128)S(1)}, ...), condition=%wide.region_11.14_spmd, body=%wide.region_10.13_spmd.sunk | while | flops 277354016 | bytes 10840809 | solution.py:132
  144.4 1.7 fusion.207
  146.1 1.4 fusion.208
  149.0 1.7 fusion.207
  150.7 1.4 fusion.208
  153.6 1.7 fusion.207
  155.3 1.4 fusion.208
  157.2 119.3 %psum.29 = bf16[64,128]{1,0:T(8,128)(2,1)S(1)} all-reduce(bf16[64,128]{1,0:T(8,128)(2,1)S(1)} %convolution_convert_fusion.2), channel_id=1, replica_groups=mesh['blk'=32,'col'=8] {'blk'}, use_global_device_ids=true, to_apply=%region_12.15 | all-reduce | flops 8192 | bytes 32768 | tf_op jit(solution)/shard_map/psum | solution.py:145
  276.6 14.8 %while.68 = (s32[]{:T(128)}, f32[2,1024]{1,0:T(2,128)S(1)}, f32[3,4,2]{1,2,0:T(2,128)S(1)}, s32[3,4]{1,0:T(4,128)S(1)}, bf16[2,1024,256]{2,1,0:T(8,128)(2,1)S(1)...) while((s32[]{:T(128)}, f32[2,1024]{1,0:T(2,128)S(1)}, ...), condition=%wide.region_14.17_spmd.clone, body=%wide.region_13.16_spmd.clone.sunk | while | flops 277455904 | bytes 10809075 | solution.py:108
  277.4 1.7 fusion.230
  279.1 2.2 fusion.231
  282.3 1.7 fusion.230
  284.0 2.2 fusion.231
  287.2 1.7 fusion.230
  289.0 2.2 fusion.231
  291.4 15.3 %psum.30 = f32[2,1024]{1,0:T(2,128)S(1)} all-reduce(f32[2,1024]{1,0:T(2,128)S(1)} %get-tuple-element.536), channel_id=1, replica_groups=mesh['blk'=32,'col'=8] {'col'}, use_global_device_ids=true, to_apply=%region_15.18 | all-reduce | flops 2048 | bytes 16384 | tf_op jit(solution)/shard_map/psum | solution.py:142
  306.7 19.8 %while.66 = (s32[]{:T(128)}, f32[3,4,128]{2,1,0:T(4,128)S(1)}, s32[3,4]{1,0:T(4,128)S(1)}, f32[2,1024]{1,0:T(2,128)S(1)}, bf16[2,1024,256]{2,1,0:T(8,128)(2,1)S(...) while((s32[]{:T(128)}, f32[3,4,128]{2,1,0:T(4,128)S(1)}, ...), condition=%wide.region_17.20_spmd, body=%wide.region_16.19_spmd.sunk | while | flops 277354016 | bytes 10840809 | solution.py:132
  307.4 2.0 gather_fusion.2
  309.5 2.3 fusion.214
  311.8 1.4 fusion.215
  314.0 2.0 gather_fusion.2
  316.0 2.3 fusion.214
  318.4 1.4 fusion.215
  320.6 2.0 gather_fusion.2
  322.6 2.3 fusion.214
  325.0 1.4 fusion.215
  326.8 124.0 %psum.31 = bf16[64,128]{1,0:T(8,128)(2,1)S(1)} all-reduce(bf16[64,128]{1,0:T(8,128)(2,1)S(1)} %convolution_convert_fusion.1), channel_id=1, replica_groups=mesh['blk'=32,'col'=8] {'blk'}, use_global_device_ids=true, to_apply=%region_18.21 | all-reduce | flops 8192 | bytes 32768 | tf_op jit(solution)/shard_map/psum | solution.py:145
  451.1 68.1 %while.69 = (s32[]{:T(128)}, f32[2,1024,256]{2,0,1:T(2,128)}, f32[3,4,128,256]{3,2,1,0:T(8,128)}, f32[3,4,2]{1,2,0:T(2,128)S(1)}, s32[3,4]{1,0:T(4,128)S(1)}, /*...) while((s32[]{:T(128)}, f32[2,1024,256]{2,0,1:T(2,128)}, ...), condition=%wide.region_20.23_spmd.clone, body=%wide.region_19.22_spmd.clone.sunk | while | flops 837293056 | bytes 54619556 | solution.py:175
  451.8 2.0 gather_fusion.8
  453.8 2.0 gather_fusion.6
  455.8 2.7 multiply_convert_fusion.2
  459.9 1.8 fusion.242
  461.7 10.7 %select_add_fusion.2 = f32[2,1024,256]{2,0,1:T(2,128)S(1)} fusion(f32[2,1024,256]{2,0,1:T(2,128)S(1)} %copy-done.1, pred[]{:T(512)S(6)} %compare.11, f32[4,1024,256]{2,1,0:T(8,128)S(1)} %fusion.242, f32[3,4,2]{1,2,0:T(2,128)S(1)} %get-tuple-element.1191, s32[]{:T(128)S(6)} %copy.139), kind=kOutput, calls=%fused_computation.139.clone.1 | convolution fusion | flops 26214400 | bytes 8389637 | tf_op jit(solution)/shard_map/while/body/eval_jaxpr/sp,sbw->pbw/dot_general | solution.py:157
  474.5 2.0 gather_fusion.8
  476.5 2.0 gather_fusion.6
  478.5 2.7 multiply_convert_fusion.2
  482.7 1.8 fusion.242
  484.5 10.7 %select_add_fusion.2 = f32[2,1024,256]{2,0,1:T(2,128)S(1)} fusion(f32[2,1024,256]{2,0,1:T(2,128)S(1)} %copy-done.1, pred[]{:T(512)S(6)} %compare.11, f32[4,1024,256]{2,1,0:T(8,128)S(1)} %fusion.242, f32[3,4,2]{1,2,0:T(2,128)S(1)} %get-tuple-element.1191, s32[]{:T(128)S(6)} %copy.139), kind=kOutput, calls=%fused_computation.139.clone.1 | convolution fusion | flops 26214400 | bytes 8389637 | tf_op jit(solution)/shard_map/while/body/eval_jaxpr/sp,sbw->pbw/dot_general | solution.py:157
  497.2 2.0 gather_fusion.8
  499.2 2.0 gather_fusion.6
  501.2 2.7 multiply_convert_fusion.2
  505.3 1.8 fusion.242
  507.1 10.7 %select_add_fusion.2 = f32[2,1024,256]{2,0,1:T(2,128)S(1)} fusion(f32[2,1024,256]{2,0,1:T(2,128)S(1)} %copy-done.1, pred[]{:T(512)S(6)} %compare.11, f32[4,1024,256]{2,1,0:T(8,128)S(1)} %fusion.242, f32[3,4,2]{1,2,0:T(2,128)S(1)} %get-tuple-element.1191, s32[]{:T(128)S(6)} %copy.139), kind=kOutput, calls=%fused_computation.139.clone.1 | convolution fusion | flops 26214400 | bytes 8389637 | tf_op jit(solution)/shard_map/while/body/eval_jaxpr/sp,sbw->pbw/dot_general | solution.py:157
  519.2 2.9 copy.96
  522.4 4.0 convolution_convert_fusion
  526.4 4.3 copy.63
  531.5 29.2 %reduce-scatter.3.cloned.1.call-done = bf16[2,128,256]{2,1,0:T(8,128)(2,1)} async-done(((bf16[2,1024,256]{2,1,0:T(8,128)(2,1)}), bf16[2,128,256]{2,1,0:T(8,128)(2,1)}) %reduce-scatter.3.cloned.1.call-update) | async-done | bytes 131088 | tf_op jit(solution)/shard_map/reduce_scatter | solution.py:177
  560.6 1.7 divide_convert_fusion.1
  562.3 90.4 %reduce-scatter.5.cloned.1.call-done = bf16[2,128,256]{2,1,0:T(8,128)(2,1)} async-done(((bf16[64,128,256]{2,1,0:T(8,128)(2,1)}), bf16[2,128,256]{2,1,0:T(8,128)(2,1)}) %reduce-scatter.5.cloned.1.call-update) | async-done | bytes 131088 | tf_op jit(solution)/shard_map/reduce_scatter | solution.py:183
  652.7 1.7 divide_convert_fusion
  (171 shorter events, 34.2 us)
Async XLA Ops:
  7.2 47.5 %all-gather.4.cloned.1.call-start = ((), (), s32[]{:S(2)}) async-start(), calls=%async_computation.2 | async-start | bytes 1179648 | tf_op jit(solution)/shard_map/all_gather | solution.py:38
  7.9 95.0 %all-gather.6.cloned.1.call-start = ((), (), s32[]{:S(2)}) async-start(), calls=%async_computation.3 | async-start | bytes 4325376 | tf_op jit(solution)/shard_map/all_gather | solution.py:68
  8.6 552.0 %reduce-scatter.3.cloned.1.call-start = ((), (), s32[]{:S(2)}) async-start(), calls=%async_computation.4 | async-start | bytes 1179648 | tf_op jit(solution)/shard_map/reduce_scatter | solution.py:177
  306.7 144.4 %copy-start = (bf16[2,1024,256]{2,1,0:T(8,128)(2,1)S(1)}, bf16[2,1024,256]{2,1,0:T(8,128)(2,1)}, u32[]{:S(2)}) copy-start(bf16[2,1024,256]{2,1,0:T(8,128)(2,1)} %all-gather.4.cloned.1.call-done) | copy-start | bytes 3145732
  455.8 2.7 copy-start.3
  459.9 1.8 copy-start.1
  472.5 1.3 copy-start.2
  478.5 2.7 copy-start.3
  482.6 1.8 copy-start.1
  495.2 1.3 copy-start.2
  501.2 2.7 copy-start.3
  505.3 1.8 copy-start.1
  517.9 1.3 copy-start.2
  519.2 3.2 copy-start.4
  522.1 130.6 %reduce-scatter.5.cloned.1.call-start = ((), (), s32[]{:S(2)}) async-start(), calls=%async_computation.5 | async-start | bytes 4325376 | tf_op jit(solution)/shard_map/reduce_scatter | solution.py:183
  530.8 0.7 copy-start.5
  530.8 0.7 copy-start.6
Sparse Core Ops, SparseCore 0:
  9.8 41.3 all-gather.3
  53.7 49.1 all-gather.5
  522.2 38.3 reduce-scatter.2
  564.4 88.2 reduce-scatter.4
where the time goes:
time: 662 us; the launch traced here: 661 us
  blocking collectives  317 us (48%)
  waiting for transfers between devices  166 us (25%)
  matrix products  105 us (16%)
  local copies, waits for them, and re-layouts  45.6 us (7%)
  between operations  14 us (2%)
  other arithmetic  11.7 us (2%)
    psum x2, blocking collectives, local(): lax.psum(col_terms.astype(jnp.bfloat16), 'blk').astype(jnp.float32)  243 us
    reduce_scatter x1, waiting for transfers between devices, local(): lax.psum_scatter(jnp.einsum('ns,stw->ntw', wanted, pair_sums, precision=h...  90.4 us
    all_gather x1, waiting for transfers between devices, local(): shard_piece = lax.all_gather(tgt_feat, 'blk', axis=0, tiled=True)  45 us
    psum x2, blocking collectives, local(): row_sums = lax.psum(row_pass(column_scaling_vector), 'col')  33 us
    dot_general x3, matrix products, final_step(): jnp.einsum('sp,sbw->pbw', onehot_slots, toward, precision=highest)  32.2 us
    dot_general x15, matrix products, kernels(): jnp.einsum('sbw,stw->sbt', src_blocks, tgt_tiles, preferred_element_type=...  30.5 us
    reduce_scatter x1, waiting for transfers between devices, local(): lax.psum_scatter(src_sums.astype(jnp.bfloat16), 'col', scatter_dimension=...  29.2 us
    all_gather x1, blocking collectives, local(): lax.all_gather(tgt_mass, 'blk', axis=0, tiled=True).astype(jnp.float32)  21.5 us
  transfers between devices with their start and end apart: 4, of which 3 were waited for; matrix products, arithmetic and copies ran while one was open for 3% of the time, Pallas kernels for 0%

commit v1 on v0

--- a/solution.py
+++ b/solution.py
@@ -142,7 +142,8 @@
         row_sums = lax.psum(row_pass(column_scaling_vector), "col")
         scaling_u = src_weight / row_sums
         col_terms = col_pass(scaling_u)
-        column_scaling_vector = masses / lax.psum(col_terms.astype(jnp.bfloat16), "blk").astype(
+        _bring_ticks = lambda patch: jnp.sum(jax.lax.all_gather(patch, "blk"), 0)
+        column_scaling_vector = masses / _bring_ticks(col_terms.astype(jnp.bfloat16)).astype(
             jnp.float32
         )
 

time: 662 us -> 464 us (0.70)
  blocking collectives: 317 us -> 121 us
    psum x2 -> x0, blocking collectives: 243 us -> none  [local(): lax.psum(col_terms.astype(jnp.bfloat16), 'blk').astype(jnp.float32)]
    all_gather x0 -> x2, blocking collectives: none -> 47.1 us  [local(): _bring_ticks = lambda patch: jnp.sum(jax.lax.all_gather(patch, 'blk'), 0)]
  transfers between devices with their start and end apart: 4 -> 4, of which waited for: 3 -> 3; matrix products, arithmetic and copies ran while one was open for 3% -> 4% of each run, Pallas kernels for 0% -> 0%
where the time goes in v1:
time: 464 us; the launch traced here: 463 us
  waiting for transfers between devices  164 us (35%)
  blocking collectives  121 us (26%)
  matrix products  105 us (23%)
  local copies, waits for them, and re-layouts  45.6 us (10%)
  between operations  14 us (3%)
  other arithmetic  11.9 us (3%)
    reduce_scatter x1, waiting for transfers between devices, local(): lax.psum_scatter(jnp.einsum('ns,stw->ntw', wanted, pair_sums, precision=h...  90.5 us
    all_gather x2, blocking collectives, local(): _bring_ticks = lambda patch: jnp.sum(jax.lax.all_gather(patch, 'blk'), 0)  47.1 us
    all_gather x1, waiting for transfers between devices, local(): shard_piece = lax.all_gather(tgt_feat, 'blk', axis=0, tiled=True)  45 us
    psum x2, blocking collectives, local(): row_sums = lax.psum(row_pass(column_scaling_vector), 'col')  33 us
    dot_general x3, matrix products, final_step(): jnp.einsum('sp,sbw->pbw', onehot_slots, toward, precision=highest)  32.2 us
    dot_general x15, matrix products, kernels(): jnp.einsum('sbw,stw->sbt', src_blocks, tgt_tiles, preferred_element_type=...  30.5 us
    reduce_scatter x1, waiting for transfers between devices, local(): lax.psum_scatter(src_sums.astype(jnp.bfloat16), 'col', scatter_dimension=...  27.2 us
    all_gather x1, blocking collectives, local(): lax.all_gather(tgt_mass, 'blk', axis=0, tiled=True).astype(jnp.float32)  21.5 us
  transfers between devices with their start and end apart: 4, of which 3 were waited for; matrix products, arithmetic and copies ran while one was open for 4% of the time, Pallas kernels for 0%

profile of v1, /device:TPU:2, one launch (start us, length us, event | category | flops | bytes accessed | tf_op | source)
XLA Modules:
  0.0 463.0 jit_solution(6371550108253398680)
XLA Ops:
  13.0 19.3 %all_gather.24 = bf16[2,1024]{1,0:T(2,128)(2,1)S(1)} all-gather(bf16[2,128]{1,0:T(2,128)(2,1)} %param.23), channel_id=1, replica_groups=mesh['blk'=32,'col'=8] {'col'}, dimensions={1}, use_global_device_ids=true | all-gather | bytes 4608 | tf_op jit(solution)/shard_map/all_gather | solution.py:39
  32.3 21.5 %all-gather.2 = bf16[32,2,128]{2,1,0:T(2,128)(2,1)S(1)} all-gather(bf16[1,2,128]{2,1,0:T(2,128)(2,1)} %bitcast.192), channel_id=1, replica_groups=mesh['blk'=32,'col'=8] {'blk'}, dimensions={0}, use_global_device_ids=true | all-gather | bytes 16896 | tf_op jit(solution)/shard_map/all_gather | solution.py:67
  54.7 1.6 fusion.129
  56.3 1.6 fusion.130
  57.9 45.0 %all-gather.8.cloned.1.call-done = bf16[64,128,256]{2,1,0:T(8,128)(2,1)} async-done(((bf16[2,128,256]{2,1,0:T(8,128)(2,1)}), bf16[64,128,256]{2,1,0:T(8,128)(2,1)}) %all-gather.8.cloned.1.call-update) | async-done | bytes 4194320 | tf_op jit(solution)/shard_map/all_gather | solution.py:68
  102.9 4.6 %fusion.131 = (f32[12,128]{0,1:T(8,128)S(1)}, bf16[12,128,256]{2,0,1:T(8,128)(2,1)S(1)}) fusion(bf16[64,128,256]{2,1,0:T(8,128)(2,1)} %all-gather.8.cloned.1.call-done, s32[12]{0:T(128)S(1)} %select_reduce_fusion), kind=kOutput, calls=%fused_computation.176 | convolution fusion | flops 51903744 | bytes 4986928 | tf_op jit(solution)/shard_map/sm,mtw->stw/dot_general | solution.py:73
  110.5 14.7 %while.67 = (s32[]{:T(128)}, f32[2,1024]{1,0:T(2,128)S(1)}, f32[3,4,2]{1,2,0:T(2,128)S(1)}, s32[3,4]{1,0:T(4,128)S(1)}, bf16[2,1024,256]{2,1,0:T(8,128)(2,1)S(1)...) while((s32[]{:T(128)}, f32[2,1024]{1,0:T(2,128)S(1)}, ...), condition=%wide.region_8.10_spmd.clone, body=%wide.region_7.9_spmd.clone.sunk | while | flops 277455904 | bytes 10809075 | solution.py:108
  111.2 1.7 fusion.222
  112.9 2.2 fusion.223
  116.1 1.7 fusion.222
  117.9 2.2 fusion.223
  121.1 1.7 fusion.222
  122.8 2.2 fusion.223
  125.2 17.7 %psum.14 = f32[2,1024]{1,0:T(2,128)S(1)} all-reduce(f32[2,1024]{1,0:T(2,128)S(1)} %get-tuple-element.534), channel_id=1, replica_groups=mesh['blk'=32,'col'=8] {'col'}, use_global_device_ids=true, to_apply=%region_9.11 | all-reduce | flops 2048 | bytes 16384 | tf_op jit(solution)/shard_map/psum | solution.py:142
  143.0 13.8 %while.65 = (s32[]{:T(128)}, f32[3,4,128]{2,1,0:T(4,128)S(1)}, s32[3,4]{1,0:T(4,128)S(1)}, f32[2,1024]{1,0:T(2,128)S(1)}, bf16[2,1024,256]{2,1,0:T(8,128)(2,1)S(...) while((s32[]{:T(128)}, f32[3,4,128]{2,1,0:T(4,128)S(1)}, ...), condition=%wide.region_11.14_spmd, body=%wide.region_10.13_spmd.sunk | while | flops 277354016 | bytes 10840809 | solution.py:132
  144.4 1.7 fusion.207
  146.1 1.4 fusion.208
  149.0 1.7 fusion.207
  150.7 1.4 fusion.208
  153.6 1.7 fusion.207
  155.3 1.4 fusion.208
  157.2 23.3 %all-gather = bf16[2048,128]{1,0:T(8,128)(2,1)S(1)} all-gather(bf16[64,128]{1,0:T(8,128)(2,1)S(1)} %convolution_convert_fusion.2), channel_id=2, replica_groups=mesh['blk'=32,'col'=8] {'blk'}, dimensions={0}, use_global_device_ids=true | all-gather | bytes 540672 | tf_op jit(solution)/shard_map/all_gather | solution.py:145
  180.8 14.8 %while.68 = (s32[]{:T(128)}, f32[2,1024]{1,0:T(2,128)S(1)}, f32[3,4,2]{1,2,0:T(2,128)S(1)}, s32[3,4]{1,0:T(4,128)S(1)}, bf16[2,1024,256]{2,1,0:T(8,128)(2,1)S(1)...) while((s32[]{:T(128)}, f32[2,1024]{1,0:T(2,128)S(1)}, ...), condition=%wide.region_14.17_spmd.clone, body=%wide.region_13.16_spmd.clone.sunk | while | flops 277455904 | bytes 10809075 | solution.py:108
  181.6 1.7 fusion.230
  183.3 2.2 fusion.231
  186.5 1.7 fusion.230
  188.2 2.2 fusion.231
  191.4 1.7 fusion.230
  193.1 2.2 fusion.231
  195.6 15.3 %psum.15 = f32[2,1024]{1,0:T(2,128)S(1)} all-reduce(f32[2,1024]{1,0:T(2,128)S(1)} %get-tuple-element.536), channel_id=1, replica_groups=mesh['blk'=32,'col'=8] {'col'}, use_global_device_ids=true, to_apply=%region_15.18 | all-reduce | flops 2048 | bytes 16384 | tf_op jit(solution)/shard_map/psum | solution.py:142
  210.9 19.8 %while.66 = (s32[]{:T(128)}, f32[3,4,128]{2,1,0:T(4,128)S(1)}, s32[3,4]{1,0:T(4,128)S(1)}, f32[2,1024]{1,0:T(2,128)S(1)}, bf16[2,1024,256]{2,1,0:T(8,128)(2,1)S(...) while((s32[]{:T(128)}, f32[3,4,128]{2,1,0:T(4,128)S(1)}, ...), condition=%wide.region_17.20_spmd, body=%wide.region_16.19_spmd.sunk | while | flops 277354016 | bytes 10840809 | solution.py:132
  211.6 2.0 gather_fusion.2
  213.6 2.3 fusion.214
  216.0 1.4 fusion.215
  218.2 2.0 gather_fusion.2
  220.2 2.3 fusion.214
  222.5 1.4 fusion.215
  224.8 2.0 gather_fusion.2
  226.8 2.3 fusion.214
  229.1 1.4 fusion.215
  231.0 23.8 %all-gather.1 = bf16[2048,128]{1,0:T(8,128)(2,1)S(1)} all-gather(bf16[64,128]{1,0:T(8,128)(2,1)S(1)} %convolution_convert_fusion.1), channel_id=3, replica_groups=mesh['blk'=32,'col'=8] {'blk'}, dimensions={0}, use_global_device_ids=true | all-gather | bytes 540672 | tf_op jit(solution)/shard_map/all_gather | solution.py:145
  255.0 68.1 %while.69 = (s32[]{:T(128)}, f32[2,1024,256]{2,0,1:T(2,128)}, f32[3,4,128,256]{3,2,1,0:T(8,128)}, f32[3,4,2]{1,2,0:T(2,128)S(1)}, s32[3,4]{1,0:T(4,128)S(1)}, /*...) while((s32[]{:T(128)}, f32[2,1024,256]{2,0,1:T(2,128)}, ...), condition=%wide.region_20.23_spmd.clone, body=%wide.region_19.22_spmd.clone.sunk | while | flops 837293056 | bytes 54619556 | solution.py:176
  255.8 2.0 gather_fusion.8
  257.8 2.0 gather_fusion.6
  259.8 2.7 multiply_convert_fusion.2
  263.9 1.8 fusion.242
  265.7 10.7 %select_add_fusion.2 = f32[2,1024,256]{2,0,1:T(2,128)S(1)} fusion(f32[2,1024,256]{2,0,1:T(2,128)S(1)} %copy-done.1, pred[]{:T(512)S(6)} %compare.11, f32[4,1024,256]{2,1,0:T(8,128)S(1)} %fusion.242, f32[3,4,2]{1,2,0:T(2,128)S(1)} %get-tuple-element.1191, s32[]{:T(128)S(6)} %copy.139), kind=kOutput, calls=%fused_computation.139.clone.1 | convolution fusion | flops 26214400 | bytes 8389637 | tf_op jit(solution)/shard_map/while/body/eval_jaxpr/sp,sbw->pbw/dot_general | solution.py:158
  278.5 2.0 gather_fusion.8
  280.5 2.0 gather_fusion.6
  282.5 2.7 multiply_convert_fusion.2
  286.6 1.8 fusion.242
  288.4 10.7 %select_add_fusion.2 = f32[2,1024,256]{2,0,1:T(2,128)S(1)} fusion(f32[2,1024,256]{2,0,1:T(2,128)S(1)} %copy-done.1, pred[]{:T(512)S(6)} %compare.11, f32[4,1024,256]{2,1,0:T(8,128)S(1)} %fusion.242, f32[3,4,2]{1,2,0:T(2,128)S(1)} %get-tuple-element.1191, s32[]{:T(128)S(6)} %copy.139), kind=kOutput, calls=%fused_computation.139.clone.1 | convolution fusion | flops 26214400 | bytes 8389637 | tf_op jit(solution)/shard_map/while/body/eval_jaxpr/sp,sbw->pbw/dot_general | solution.py:158
  301.2 2.0 gather_fusion.8
  303.2 2.0 gather_fusion.6
  305.2 2.7 multiply_convert_fusion.2
  309.3 1.8 fusion.242
  311.1 10.7 %select_add_fusion.2 = f32[2,1024,256]{2,0,1:T(2,128)S(1)} fusion(f32[2,1024,256]{2,0,1:T(2,128)S(1)} %copy-done.1, pred[]{:T(512)S(6)} %compare.11, f32[4,1024,256]{2,1,0:T(8,128)S(1)} %fusion.242, f32[3,4,2]{1,2,0:T(2,128)S(1)} %get-tuple-element.1191, s32[]{:T(128)S(6)} %copy.139), kind=kOutput, calls=%fused_computation.139.clone.1 | convolution fusion | flops 26214400 | bytes 8389637 | tf_op jit(solution)/shard_map/while/body/eval_jaxpr/sp,sbw->pbw/dot_general | solution.py:158
  323.2 2.9 copy.96
  326.4 4.0 convolution_convert_fusion
  330.4 4.3 copy.63
  335.4 27.2 %reduce-scatter.3.cloned.1.call-done = bf16[2,128,256]{2,1,0:T(8,128)(2,1)} async-done(((bf16[2,1024,256]{2,1,0:T(8,128)(2,1)}), bf16[2,128,256]{2,1,0:T(8,128)(2,1)}) %reduce-scatter.3.cloned.1.call-update) | async-done | bytes 131088 | tf_op jit(solution)/shard_map/reduce_scatter | solution.py:178
  362.6 1.7 divide_convert_fusion.1
  364.3 90.5 %reduce-scatter.5.cloned.1.call-done = bf16[2,128,256]{2,1,0:T(8,128)(2,1)} async-done(((bf16[64,128,256]{2,1,0:T(8,128)(2,1)}), bf16[2,128,256]{2,1,0:T(8,128)(2,1)}) %reduce-scatter.5.cloned.1.call-update) | async-done | bytes 131088 | tf_op jit(solution)/shard_map/reduce_scatter | solution.py:184
  454.8 1.7 divide_convert_fusion
  (173 shorter events, 34.4 us)
Async XLA Ops:
  7.2 47.5 %all-gather.6.cloned.1.call-start = ((), (), s32[]{:S(2)}) async-start(), calls=%async_computation.2 | async-start | bytes 1179648 | tf_op jit(solution)/shard_map/all_gather | solution.py:38
  7.9 95.0 %all-gather.8.cloned.1.call-start = ((), (), s32[]{:S(2)}) async-start(), calls=%async_computation.3 | async-start | bytes 4325376 | tf_op jit(solution)/shard_map/all_gather | solution.py:68
  8.6 354.0 %reduce-scatter.3.cloned.1.call-start = ((), (), s32[]{:S(2)}) async-start(), calls=%async_computation.4 | async-start | bytes 1179648 | tf_op jit(solution)/shard_map/reduce_scatter | solution.py:178
  210.9 44.2 %copy-start = (bf16[2,1024,256]{2,1,0:T(8,128)(2,1)S(1)}, bf16[2,1024,256]{2,1,0:T(8,128)(2,1)}, u32[]{:S(2)}) copy-start(bf16[2,1024,256]{2,1,0:T(8,128)(2,1)} %all-gather.6.cloned.1.call-done) | copy-start | bytes 3145732
  259.8 2.7 copy-start.3
  263.9 1.8 copy-start.1
  276.5 1.3 copy-start.2
  282.5 2.7 copy-start.3
  286.6 1.8 copy-start.1
  299.2 1.3 copy-start.2
  305.2 2.7 copy-start.3
  309.3 1.8 copy-start.1
  321.8 1.3 copy-start.2
  323.2 3.2 copy-start.4
  326.1 128.7 %reduce-scatter.5.cloned.1.call-start = ((), (), s32[]{:S(2)}) async-start(), calls=%async_computation.5 | async-start | bytes 4325376 | tf_op jit(solution)/shard_map/reduce_scatter | solution.py:184
  334.8 0.7 copy-start.5
  334.8 0.7 copy-start.6
Sparse Core Ops, SparseCore 0:
  9.8 41.3 all-gather.5
  53.7 49.1 all-gather.7
  326.2 36.3 reduce-scatter.2
  366.4 88.3 reduce-scatter.4
